TPU v7x, 512 devices: a whole 4x8x8 slice. The times are simulated.
512 devices in a mesh: dp: 8 (over y), seq: 64 (over z, x, core).
Axes of the slice: x: 4, y: 8, z: 8, core: 2. Of those that a mesh axis runs over, the one named last changes fastest.
Arguments:
- queries: bfloat16 [8, 8192, 1536], P('dp', 'seq'), may hold values from -6 to 6
- keys: bfloat16 [8, 8192, 1536], P('dp', 'seq'), may hold values from -6 to 6
- values: bfloat16 [8, 8192, 1536], P('dp', 'seq'), may hold values from -6 to 6
- segment_ids: int32 [8, 8192], P('dp'), may hold values from 0 to 127, never falling along the last dimension, each value on 1 to 128 neighbouring positions
- norm_gain: float32 [1536], replicated, may hold values from 0.25 to 1.75
- conv_kernel: float32 [31, 1536], replicated, may hold values from -1 to 1
- conv_bias: float32 [1536], replicated, may hold values from -3 to 3
- cotangent: bfloat16 [8, 8192, 1536], P('dp', 'seq'), may hold values from -6 to 6
Outputs:
- conv_out: bfloat16 [8, 8192, 1536], P('dp', 'seq')
- query_grad: bfloat16 [8, 8192, 1536], P('dp', 'seq')
- key_grad: bfloat16 [8, 8192, 1536], P('dp', 'seq')
- value_grad: bfloat16 [8, 8192, 1536], P('dp', 'seq')
- gain_grad: float32 [1536], replicated
- kernel_grad: float32 [31, 1536], replicated
- bias_grad: float32 [1536], replicated
Inputs may be any that keep to these rules, and one draw needn't show every extreme that they name: `segment_ids`: within each row, utterance numbers never fall; each utterance holds 1 to 128 frames, and some utterance exactly 128.
All inputs are finite; a program needn't handle non-finite values.
Results may differ from a plain program's by a relative error of at most 0.023.
Values may be sent and summed in bfloat16 or wider, within the bound.
A program may use at most 64 MiB of HBM per device.

v0:
```python
import jax
import jax.numpy as jnp
from jax import lax
from jax.sharding import PartitionSpec as P

HEADS = 24
HEAD_DIM = 64
HEAD_BLOCK = 4
REACH = 1
EPS = 1e-05
NEG = -1e30


def shifted(block, axis, distance):
    devices = range(lax.axis_size(axis))
    route = [(i - distance, i) for i in devices if i - distance in devices]
    return lax.ppermute(block, axis, route)


def with_halo(cells, sides, width):
    for axis, dim in sides:
        count = lax.axis_size(axis)
        ends = count - 1
        head = lax.slice_in_dim(cells, 0, width, axis=dim)
        tail = lax.slice_in_dim(cells, cells.shape[dim] - width, cells.shape[dim], axis=dim)
        cells = jnp.concatenate(
            [
                lax.ppermute(tail, axis, [(i, (i + 1) % count) for i in range(ends)]),
                cells,
                lax.ppermute(head, axis, [((i + 1) % count, i) for i in range(ends)]),
            ],
            axis=dim,
        )
    return cells


def to_groups(tensor, block):
    rows_in, heads_in, dim_in = tensor.shape
    return tensor.reshape(rows_in, heads_in // block, block, dim_in).transpose(1, 0, 2, 3)


def from_groups(tensor):
    groups_in, rows_in, block, dim_in = tensor.shape
    return tensor.transpose(1, 0, 2, 3).reshape(rows_in, groups_in * block * dim_in)


def masked_logits(query_rows, key_rows, same_seg):
    factor = query_rows.shape[-1] ** (-0.5)
    logits = (
        jnp.einsum("qhe,khe->hqk", query_rows, key_rows, preferred_element_type=jnp.float32)
        * factor
    )
    return jnp.where(same_seg[None], logits, NEG)


def forward_block(query_rows, key_rows, value_rows, same_seg):
    logits = masked_logits(query_rows, key_rows, same_seg)
    row_top = jnp.max(logits, -1, keepdims=True)
    exponent = jnp.exp(logits - row_top)
    row_total = jnp.sum(exponent, -1, keepdims=True)
    attn_weights = (exponent / row_total).astype(jnp.bfloat16)
    context = jnp.einsum(
        "hqk,khe->qhe", attn_weights, value_rows, preferred_element_type=jnp.float32
    )
    return (context, (row_top + jnp.log(row_total))[..., 0])


def back_terms(query_rows, key_rows, value_rows, grad_rows, log_total, row_delta, same_seg):
    factor = query_rows.shape[-1] ** (-0.5)
    logits = masked_logits(query_rows, key_rows, same_seg)
    prob_back = jnp.exp(logits - log_total[:, :, None])
    grad_prob = jnp.einsum(
        "qhe,khe->hqk", grad_rows, value_rows, preferred_element_type=jnp.float32
    )
    grad_logit = (prob_back * (grad_prob - row_delta[:, :, None]) * factor).astype(jnp.bfloat16)
    return (prob_back.astype(jnp.bfloat16), grad_logit)


def per_device(queries, keys, values, segment_ids, norm_gain, conv_kernel, conv_bias, cotangent):
    frame_count = queries.shape[1]
    width = queries.shape[2]
    reach_rows = REACH * frame_count
    tap_count = conv_kernel.shape[0]
    half_taps = tap_count // 2
    block = HEAD_BLOCK
    group_count = HEADS // block
    start_row = lax.axis_index("seq") * frame_count
    seg_row = segment_ids[0]
    seg_padded = jnp.pad(seg_row, (reach_rows, reach_rows), constant_values=-1)
    own_seg = lax.dynamic_slice_in_dim(seg_row, start_row, frame_count)
    window_seg = lax.dynamic_slice_in_dim(seg_padded, start_row, frame_count + 2 * reach_rows)
    conv_seg = lax.dynamic_slice_in_dim(
        seg_padded, start_row + reach_rows - half_taps, frame_count + 2 * half_taps
    )
    same_fwd = own_seg[:, None] == window_seg[None, :]
    query_heads = queries[0].reshape(frame_count, HEADS, HEAD_DIM)
    key_value = jnp.stack((keys[0], values[0]), 1)
    lower_parts = []
    upper_parts = []
    hop = 1
    for offset_by in (hop, -hop):
        arrived = shifted(key_value, "seq", offset_by)
        if offset_by > 0:
            lower_parts.insert(0, arrived)
        else:
            upper_parts.append(arrived)
    key_value_wide = jnp.concatenate(lower_parts + [key_value] + upper_parts, 0)
    query_groups = to_groups(query_heads, block)
    key_groups = to_groups(key_value_wide[:, 0].reshape(-1, HEADS, HEAD_DIM), block)
    value_groups = to_groups(key_value_wide[:, 1].reshape(-1, HEADS, HEAD_DIM), block)

    def forward_group(operands):
        return forward_block(operands[0], operands[1], operands[2], same_fwd)

    context_groups, total_groups = lax.map(forward_group, (query_groups, key_groups, value_groups))
    context = from_groups(context_groups).astype(jnp.bfloat16)
    context_f = context.astype(jnp.float32)
    row_mean = jnp.mean(context_f, -1, keepdims=True)
    centred = context_f - row_mean
    inv_std = lax.rsqrt(jnp.mean(centred * centred, -1, keepdims=True) + EPS)
    normed = centred * inv_std
    conv_in = (normed * norm_gain).astype(jnp.bfloat16)
    conv_wide = with_halo(conv_in, (("seq", 0),), half_taps).astype(jnp.float32)
    same_taps = [
        (conv_seg[tap_index : tap_index + frame_count] == own_seg)[:, None]
        for tap_index in range(tap_count)
    ]
    pre_act = jnp.broadcast_to(conv_bias, (frame_count, width))
    for tap_index in range(tap_count):
        pre_act = pre_act + conv_kernel[tap_index] * jnp.where(
            same_taps[tap_index], conv_wide[tap_index : tap_index + frame_count], 0.0
        )
    gate_sig = jax.nn.sigmoid(pre_act)
    conv_out = (pre_act * gate_sig).astype(jnp.bfloat16)
    grad_pre = (
        cotangent[0].astype(jnp.float32) * gate_sig * (1.0 + pre_act * (1.0 - gate_sig))
    ).astype(jnp.bfloat16)
    grad_pre_f = grad_pre.astype(jnp.float32)
    bias_part = jnp.sum(grad_pre_f, 0)
    kernel_rows = []
    for tap_index in range(tap_count):
        kernel_rows.append(
            jnp.sum(
                jnp.where(
                    same_taps[tap_index],
                    conv_wide[tap_index : tap_index + frame_count] * grad_pre_f,
                    0.0,
                ),
                0,
            )
        )
    kernel_part = jnp.stack(kernel_rows, 0)
    grad_wide = with_halo(grad_pre, (("seq", 0),), half_taps).astype(jnp.float32)
    grad_in = jnp.zeros((frame_count, width), jnp.float32)
    for tap_index in range(tap_count):
        mirror = 2 * half_taps - tap_index
        grad_in = grad_in + conv_kernel[tap_index] * jnp.where(
            same_taps[mirror], grad_wide[mirror : mirror + frame_count], 0.0
        )
    gain_part = jnp.sum(grad_in * normed, 0)
    grad_norm = grad_in * norm_gain
    grad_context = (
        (
            grad_norm
            - jnp.mean(grad_norm, -1, keepdims=True)
            - normed * jnp.mean(grad_norm * normed, -1, keepdims=True)
        )
        * inv_std
    ).astype(jnp.bfloat16)
    row_delta = jnp.sum(
        (grad_context.astype(jnp.float32) * context_f).reshape(frame_count, HEADS, HEAD_DIM), -1
    )
    delta_groups = row_delta.T.reshape(group_count, block, frame_count)
    grad_groups = to_groups(grad_context.reshape(frame_count, HEADS, HEAD_DIM), block)

    def backward_group(operands):
        query_rows, key_rows, value_rows, grad_rows, log_total, delta_rows = operands
        prob_low, grad_logit = back_terms(
            query_rows, key_rows, value_rows, grad_rows, log_total, delta_rows, same_fwd
        )
        query_part = jnp.einsum(
            "hqk,khe->qhe", grad_logit, key_rows, preferred_element_type=jnp.float32
        )
        key_part = jnp.einsum(
            "hqk,qhe->khe", grad_logit, query_rows, preferred_element_type=jnp.float32
        )
        value_part = jnp.einsum(
            "hqk,qhe->khe", prob_low, grad_rows, preferred_element_type=jnp.float32
        )
        return (query_part, key_part, value_part)

    query_blocks, key_blocks, value_blocks = lax.map(
        backward_group,
        (query_groups, key_groups, value_groups, grad_groups, total_groups, delta_groups),
    )
    key_value_grad = jnp.stack((from_groups(key_blocks), from_groups(value_blocks)), 1)
    own_grad = key_value_grad[reach_rows : reach_rows + frame_count]
    hop = 1
    for offset_by in (hop, -hop):
        if offset_by > 0:
            moved_piece = key_value_grad[
                (REACH + hop) * frame_count : (REACH + hop + 1) * frame_count
            ]
        else:
            moved_piece = key_value_grad[
                (REACH - hop) * frame_count : (REACH - hop + 1) * frame_count
            ]
        own_grad = own_grad + shifted(moved_piece.astype(jnp.bfloat16), "seq", offset_by).astype(
            moved_piece.dtype
        )
    key_grad = own_grad[:, 0]
    value_grad = own_grad[:, 1]
    query_grad = from_groups(query_blocks)
    gain_sum, kernel_sum, bias_sum = lax.psum((gain_part, kernel_part, bias_part), ("dp", "seq"))
    norm_factor = (lax.axis_size("dp") * lax.axis_size("seq") * frame_count) ** (-0.5)
    return (
        conv_out[None],
        query_grad.astype(jnp.bfloat16)[None],
        key_grad.astype(jnp.bfloat16)[None],
        value_grad.astype(jnp.bfloat16)[None],
        gain_sum * norm_factor,
        kernel_sum * norm_factor,
        bias_sum * norm_factor,
    )


def solution(mesh):
    placed = (
        P("dp", "seq", None),
        P("dp", "seq", None),
        P("dp", "seq", None),
        P("dp", None),
        P(),
        P(),
        P(),
        P("dp", "seq", None),
    )
    return jax.shard_map(
        per_device,
        mesh=mesh,
        in_specs=placed,
        out_specs=(
            P("dp", "seq", None),
            P("dp", "seq", None),
            P("dp", "seq", None),
            P("dp", "seq", None),
            P(),
            P(),
            P(),
        ),
        check_vma=False,
    )
```

profile of v0, /device:TPU:1, one launch (start us, length us, event | category | flops | bytes accessed | tf_op | source)
XLA Modules:
  0.0 418.6 jit_solution(15522786637393165617)
XLA Ops:
  7.2 1.3 pad_maximum_fusion.2
  8.5 8.7 %collective-permute-start.1 = (bf16[128,2,1536]{2,0,1:T(8,128)(2,1)S(1)}, bf16[128,2,1536]{2,0,1:T(8,128)(2,1)S(1)}, u32[]{:S(2)}, u32[]{:S(2)}) collective-permute-start(bf16[128,2,1536]{2,0,1:T(8,128)(2,1)S(1)} %pad_maximum_fusion.2), channel_id=1, source_target_pairs={{1,0},{2,1},{3,2},{4,3},{5,4},{6,5},{7,6},{8,7},{9,8},{10,9},{11,1... | collective-permute-start | bytes 2359304 | tf_op jit(solution)/shard_map/ppermute | solution.py:17
  17.3 1.9 collective-permute-start
  19.2 2.5 slice_reduce_fusion.30
  26.3 1.8 collective-permute-done
  29.2 1.4 copy.23
  30.7 21.4 %while.28 = (s32[]{:T(128)}, bf16[6,128,4,64]{1,3,2,0:T(8,128)(2,1)S(1)}, f32[6,4,128]{2,1,0:T(4,128)}, bf16[6,384,4,64]{1,3,2,0:T(8,128)(2,1)}, bf16[6,128,4,64...) while((s32[]{:T(128)}, ...), condition=%wide.region_3.4_spmd.clone, body=%wide.region_0.3_spmd.clone.sunk | while | flops 51953152 | bytes 3068009 | solution.py:115
  30.8 1.2 fusion.223
  32.4 1.3 fusion.225
  34.4 1.2 fusion.223
  35.9 1.3 fusion.225
  37.9 1.2 fusion.223
  39.5 1.3 fusion.225
  41.5 1.2 fusion.223
  43.0 1.3 fusion.225
  45.1 1.2 fusion.223
  46.6 1.3 fusion.225
  48.6 1.2 fusion.223
  50.2 1.3 fusion.225
  53.9 4.4 %collective-permute-start.2 = (bf16[15,1536]{0,1:T(8,128)(2,1)}, bf16[15,1536]{0,1:T(8,128)(2,1)}, u32[]{:S(2)}, u32[]{:S(2)}) collective-permute-start(bf16[15,1536]{0,1:T(8,128)(2,1)} %get-tuple-element.291), channel_id=1, source_target_pairs={{0,1},{1,2},{2,3},{3,4},{4,5},{5,6},{6,7},{7,8},{8,9},{9,10},{10,1... | collective-permute-start | bytes 138248 | tf_op jit(solution)/shard_map/ppermute | solution.py:28
  58.3 2.1 collective-permute-start.3
  60.4 2.1 slice_reduce_fusion.29
  64.1 3.6 collective-permute-done.3
  67.7 1.6 maximum_convert_fusion
  69.6 18.6 %fusion.110 = (f32[1536]{0:T(1024)S(1)}, f32[1536]{0:T(1024)S(1)}, f32[1536]{0:T(1024)S(1)}, f32[1536]{0:T(1024)S(1)}, f32[1536]{0:T(1024)S(1)}, /*index=5*/f32[...) fusion(f32[158,1536]{0,1:T(8,128)S(1)} %maximum_convert_fusion,, ...), kind=kLoop, calls=%fused_computation.158 | loop fusion | flops 25741824 | bytes 26208128 | tf_op jit(solution)/shard_map/reduce_sum | solution.py:143
  88.3 4.4 %fusion.112 = (f32[1536]{0:T(1024)S(1)}, f32[1536]{0:T(1024)S(1)}, f32[1536]{0:T(1024)S(1)}, f32[1536]{0:T(1024)S(1)}, f32[1536]{0:T(1024)S(1)}, /*index=5*/f32[...) fusion(bf16[128,1536]{0,1:T(8,128)(2,1)S(1)} %get-tuple-element.272, ...), kind=kLoop, calls=%fused_computation.160 | loop fusion | flops 5491200 | bytes 7527552 | tf_op jit(solution)/shard_map/reduce_sum | solution.py:143
  92.8 3.7 fusion.114
  97.5 1.9 collective-permute-start.4
  99.4 3.4 collective-permute-start.5
  102.8 2.2 fusion.108
  123.5 6.0 %stack.135 = f32[31,1536]{1,0:T(8,128)} concatenate(f32[1,1536]{1,0:T(1,128)} %stack.104, f32[1,1536]{1,0:T(1,128)} %stack.105, f32[1,1536]{1,0:T(1,128)} %stack.106, f32[1,1536]{1,0:T(1,128)} %stack.107, f32[1,1536]{1,0:T(1,128)} %stack.108, f32[1,1536]{1,0:T(1,128)} %stack.109, f32[1,1536]{1,0:T(1,128)} %stack.110, f32[1,1536]{1,0:T(1,128)} %stack.111, f32[1,1536]{1,0:T(1,128)} %stack.112, ...), dimensions={0} | concatenate | bytes 380928 | tf_op jit(solution)/shard_map/stack | solution.py:152
  129.5 1.6 maximum_convert_fusion.1
  131.1 19.2 %fusion.190 = (f32[1536]{0:T(1024)}, f32[128]{0:T(128)S(1)}, f32[128]{0:T(128)S(1)}, f32[128,1536]{0,1:T(8,128)S(1)}) fusion(bf16[6,128,4,64]{1,3,2,0:T(8,128)(2,1)S(1)} %get-tuple-element.104, f32[128]{0:T(128)} %copy-done.59, f32[128]{0:T(128)} %copy-done.57, f32[1536]{0:T(1024)} %param.16, f32[158,1536]{0,1:T(8,128)S(1)} %maximum_convert_fusion.1, ...), kind=kLoop, calls=%fused_computation.277 | loop fusion | flops 19855616 | bytes 25767808 | tf_op jit(solution)/shard_map/reduce_sum | solution.py:160
  152.1 45.3 %while.29 = (s32[]{:T(128)}, bf16[6,128,4,64]{1,3,2,0:T(8,128)(2,1)S(1)}, f32[6,384,4,64]{1,3,2,0:T(8,128)}, f32[6,384,4,64]{1,3,2,0:T(8,128)S(1)}, bf16[6,384,4...) while((s32[]{:T(128)}, ...), condition=%wide.region_10.11_spmd.clone, body=%wide.region_9.10_spmd.clone.sunk | while | flops 127451136 | bytes 5426313 | solution.py:192
  152.9 1.3 fusion.237
  154.3 1.3 fusion.238
  155.6 1.2 fusion.239
  157.9 1.8 fusion.240
  160.5 1.3 fusion.237
  161.8 1.3 fusion.238
  163.1 1.2 fusion.239
  165.4 1.8 fusion.240
  168.0 1.3 fusion.237
  169.3 1.3 fusion.238
  172.9 1.8 fusion.240
  175.5 1.3 fusion.237
  176.9 1.3 fusion.238
  178.2 1.2 fusion.239
  180.5 1.8 fusion.240
  183.1 1.3 fusion.237
  184.4 1.3 fusion.238
  185.7 1.2 fusion.239
  188.0 1.8 fusion.240
  190.6 1.3 fusion.237
  192.0 1.3 fusion.238
  195.6 1.8 fusion.240
  197.4 2.0 fusion.48
  199.4 1.5 fusion.196
  200.9 2.5 collective-permute-start.6
  203.5 2.8 collective-permute-start.7
  207.4 113.5 %all-reduce.1 = (f32[1536]{0:T(1024)S(1)}, f32[1536]{0:T(1024)S(1)}) all-reduce(f32[1536]{0:T(1024)S(1)} %copy-done.39, f32[1536]{0:T(1024)S(1)} %copy-done.38), channel_id=1, replica_groups=mesh['dp'=8,'seq'=64] {'dp','seq'}, use_global_device_ids=true, to_apply=%region_12.13 | all-reduce | flops 3072 | bytes 24576 | tf_op jit(solution)/shard_map/psum | solution.py:214
  322.4 83.9 %all-reduce.4.cloned.1.call-done = f32[31,1536]{1,0:T(8,128)} async-done(((f32[31,1536]{1,0:T(8,128)}), f32[31,1536]{1,0:T(8,128)}) %all-reduce.4.cloned.1.call-update) | async-done | bytes 190480 | tf_op jit(solution)/shard_map/psum | solution.py:214
  406.3 1.6 broadcast_multiply_fusion
  407.9 1.9 fusion.52
  (231 shorter events, 54.3 us)
Async XLA Ops:
  7.2 21.0 %copy-start.2 = (bf16[1,128,1536]{2,1,0:T(8,128)(2,1)S(1)}, bf16[1,128,1536]{2,1,0:T(8,128)(2,1)}, u32[]{:S(2)}) copy-start(bf16[1,128,1536]{2,1,0:T(8,128)(2,1)} %param.14) | copy-start | bytes 1179652
  7.2 21.0 %copy-start.3 = (bf16[1,128,1536]{2,1,0:T(8,128)(2,1)S(1)}, bf16[1,128,1536]{2,1,0:T(8,128)(2,1)}, u32[]{:S(2)}) copy-start(bf16[1,128,1536]{2,1,0:T(8,128)(2,1)} %param.13) | copy-start | bytes 1179652
  7.2 15.3 %copy-start.4 = (bf16[1,128,1536]{2,1,0:T(8,128)(2,1)S(1)}, bf16[1,128,1536]{2,1,0:T(8,128)(2,1)}, u32[]{:S(2)}) copy-start(bf16[1,128,1536]{2,1,0:T(8,128)(2,1)} %param.12) | copy-start | bytes 1179652
  7.2 399.1 %all-reduce.4.cloned.1.call-start = ((), (), s32[]{:S(2)}) async-start(), calls=%async_computation | async-start | bytes 393216 | tf_op jit(solution)/shard_map/psum | solution.py:214
  8.5 17.8 %collective-permute-start.1 = (bf16[128,2,1536]{2,0,1:T(8,128)(2,1)S(1)}, bf16[128,2,1536]{2,0,1:T(8,128)(2,1)S(1)}, u32[]{:S(2)}, u32[]{:S(2)}) collective-permute-start(bf16[128,2,1536]{2,0,1:T(8,128)(2,1)S(1)} %pad_maximum_fusion.2), channel_id=1, source_target_pairs={{1,0},{2,1},{3,2},{4,3},{5,4},{6,5},{7,6},{8,7},{9,8},{10,9},{11,1... | collective-permute-start | bytes 2359304 | tf_op jit(solution)/shard_map/ppermute | solution.py:17
  17.3 10.8 %collective-permute-start = (bf16[128,2,1536]{2,0,1:T(8,128)(2,1)S(1)}, bf16[128,2,1536]{2,0,1:T(8,128)(2,1)S(1)}, u32[]{:S(2)}, u32[]{:S(2)}) collective-permute-start(bf16[128,2,1536]{2,0,1:T(8,128)(2,1)S(1)} %pad_maximum_fusion.2), channel_id=1, source_target_pairs={{0,1},{1,2},{2,3},{3,4},{4,5},{5,6},{6,7},{7,8},{8,9},{9,10},{10,1... | collective-permute-start | bytes 2359304 | tf_op jit(solution)/shard_map/ppermute | solution.py:17
  30.7 21.8 %copy-start.5 = (f32[1536]{0:T(1024)S(1)}, f32[1536]{0:T(1024)}, u32[]{:S(2)}) copy-start(f32[1536]{0:T(1024)} %param.16) | copy-start | bytes 18436
  52.3 8.1 %copy-start.57 = (f32[128]{0:T(128)}, f32[128]{0:T(128)S(1)}, u32[]{:S(2)}) copy-start(f32[128]{0:T(128)S(1)} %broadcast_multiply_fusion.5) | copy-start | bytes 1540
  52.5 7.8 %copy-start.59 = (f32[128]{0:T(128)}, f32[128]{0:T(128)S(1)}, u32[]{:S(2)}) copy-start(f32[128]{0:T(128)S(1)} %add_rsqrt_fusion) | copy-start | bytes 1540
  53.9 10.2 %collective-permute-start.2 = (bf16[15,1536]{0,1:T(8,128)(2,1)}, bf16[15,1536]{0,1:T(8,128)(2,1)}, u32[]{:S(2)}, u32[]{:S(2)}) collective-permute-start(bf16[15,1536]{0,1:T(8,128)(2,1)} %get-tuple-element.291), channel_id=1, source_target_pairs={{0,1},{1,2},{2,3},{3,4},{4,5},{5,6},{6,7},{7,8},{8,9},{9,10},{10,1... | collective-permute-start | bytes 138248 | tf_op jit(solution)/shard_map/ppermute | solution.py:28
  58.3 9.4 %collective-permute-start.3 = (bf16[15,1536]{0,1:T(8,128)(2,1)}, bf16[15,1536]{0,1:T(8,128)(2,1)}, u32[]{:S(2)}, u32[]{:S(2)}) collective-permute-start(bf16[15,1536]{0,1:T(8,128)(2,1)} %get-tuple-element.292), channel_id=1, source_target_pairs={{1,0},{2,1},{3,2},{4,3},{5,4},{6,5},{7,6},{8,7},{9,8},{10,9},{11,1... | collective-permute-start | bytes 138248 | tf_op jit(solution)/shard_map/ppermute | solution.py:30
  63.7 5.6 %copy-start.7 = (f32[1536]{0:T(1024)S(1)}, f32[1536]{0:T(1024)}, u32[]{:S(2)}) copy-start(f32[1536]{0:T(1024)} %get-tuple-element.199) | copy-start | bytes 18436
  63.7 5.6 %copy-start.8 = (f32[1536]{0:T(1024)S(1)}, f32[1536]{0:T(1024)}, u32[]{:S(2)}) copy-start(f32[1536]{0:T(1024)} %get-tuple-element.200) | copy-start | bytes 18436
  63.7 5.6 %copy-start.9 = (f32[1536]{0:T(1024)S(1)}, f32[1536]{0:T(1024)}, u32[]{:S(2)}) copy-start(f32[1536]{0:T(1024)} %get-tuple-element.201) | copy-start | bytes 18436
  63.7 5.6 %copy-start.10 = (f32[1536]{0:T(1024)S(1)}, f32[1536]{0:T(1024)}, u32[]{:S(2)}) copy-start(f32[1536]{0:T(1024)} %get-tuple-element.202) | copy-start | bytes 18436
  63.7 5.6 %copy-start.11 = (f32[1536]{0:T(1024)S(1)}, f32[1536]{0:T(1024)}, u32[]{:S(2)}) copy-start(f32[1536]{0:T(1024)} %get-tuple-element.203) | copy-start | bytes 18436
  63.7 5.6 %copy-start.12 = (f32[1536]{0:T(1024)S(1)}, f32[1536]{0:T(1024)}, u32[]{:S(2)}) copy-start(f32[1536]{0:T(1024)} %get-tuple-element.204) | copy-start | bytes 18436
  63.7 5.6 %copy-start.13 = (f32[1536]{0:T(1024)S(1)}, f32[1536]{0:T(1024)}, u32[]{:S(2)}) copy-start(f32[1536]{0:T(1024)} %get-tuple-element.205) | copy-start | bytes 18436
  63.8 5.6 %copy-start.14 = (f32[1536]{0:T(1024)S(1)}, f32[1536]{0:T(1024)}, u32[]{:S(2)}) copy-start(f32[1536]{0:T(1024)} %get-tuple-element.206) | copy-start | bytes 18436
  63.8 5.6 %copy-start.15 = (f32[1536]{0:T(1024)S(1)}, f32[1536]{0:T(1024)}, u32[]{:S(2)}) copy-start(f32[1536]{0:T(1024)} %get-tuple-element.207) | copy-start | bytes 18436
  63.8 5.6 %copy-start.16 = (f32[1536]{0:T(1024)S(1)}, f32[1536]{0:T(1024)}, u32[]{:S(2)}) copy-start(f32[1536]{0:T(1024)} %get-tuple-element.208) | copy-start | bytes 18436
  63.8 5.6 %copy-start.17 = (f32[1536]{0:T(1024)S(1)}, f32[1536]{0:T(1024)}, u32[]{:S(2)}) copy-start(f32[1536]{0:T(1024)} %get-tuple-element.209) | copy-start | bytes 18436
  63.8 5.6 %copy-start.18 = (f32[1536]{0:T(1024)S(1)}, f32[1536]{0:T(1024)}, u32[]{:S(2)}) copy-start(f32[1536]{0:T(1024)} %get-tuple-element.210) | copy-start | bytes 18436
  63.8 5.6 %copy-start.19 = (f32[1536]{0:T(1024)S(1)}, f32[1536]{0:T(1024)}, u32[]{:S(2)}) copy-start(f32[1536]{0:T(1024)} %get-tuple-element.211) | copy-start | bytes 18436
  63.8 5.6 %copy-start.20 = (f32[1536]{0:T(1024)S(1)}, f32[1536]{0:T(1024)}, u32[]{:S(2)}) copy-start(f32[1536]{0:T(1024)} %get-tuple-element.212) | copy-start | bytes 18436
  63.8 5.6 %copy-start.21 = (f32[1536]{0:T(1024)S(1)}, f32[1536]{0:T(1024)}, u32[]{:S(2)}) copy-start(f32[1536]{0:T(1024)} %get-tuple-element.213) | copy-start | bytes 18436
  63.8 5.6 %copy-start.22 = (f32[1536]{0:T(1024)S(1)}, f32[1536]{0:T(1024)}, u32[]{:S(2)}) copy-start(f32[1536]{0:T(1024)} %get-tuple-element.214) | copy-start | bytes 18436
  63.8 5.6 %copy-start.23 = (f32[1536]{0:T(1024)S(1)}, f32[1536]{0:T(1024)}, u32[]{:S(2)}) copy-start(f32[1536]{0:T(1024)} %get-tuple-element.215) | copy-start | bytes 18436
  63.9 5.6 %copy-start.24 = (f32[1536]{0:T(1024)S(1)}, f32[1536]{0:T(1024)}, u32[]{:S(2)}) copy-start(f32[1536]{0:T(1024)} %get-tuple-element.216) | copy-start | bytes 18436
  63.9 5.6 %copy-start.25 = (f32[1536]{0:T(1024)S(1)}, f32[1536]{0:T(1024)}, u32[]{:S(2)}) copy-start(f32[1536]{0:T(1024)} %get-tuple-element.217) | copy-start | bytes 18436
  63.9 5.6 %copy-start.26 = (f32[1536]{0:T(1024)S(1)}, f32[1536]{0:T(1024)}, u32[]{:S(2)}) copy-start(f32[1536]{0:T(1024)} %get-tuple-element.218) | copy-start | bytes 18436
  63.9 5.5 %copy-start.27 = (f32[1536]{0:T(1024)S(1)}, f32[1536]{0:T(1024)}, u32[]{:S(2)}) copy-start(f32[1536]{0:T(1024)} %get-tuple-element.219) | copy-start | bytes 18436
  63.9 5.5 %copy-start.28 = (f32[1536]{0:T(1024)S(1)}, f32[1536]{0:T(1024)}, u32[]{:S(2)}) copy-start(f32[1536]{0:T(1024)} %get-tuple-element.220) | copy-start | bytes 18436
  63.9 5.5 %copy-start.29 = (f32[1536]{0:T(1024)S(1)}, f32[1536]{0:T(1024)}, u32[]{:S(2)}) copy-start(f32[1536]{0:T(1024)} %get-tuple-element.221) | copy-start | bytes 18436
  63.9 5.5 %copy-start.30 = (f32[1536]{0:T(1024)S(1)}, f32[1536]{0:T(1024)}, u32[]{:S(2)}) copy-start(f32[1536]{0:T(1024)} %get-tuple-element.222) | copy-start | bytes 18436
  63.9 5.5 %copy-start.31 = (f32[1536]{0:T(1024)S(1)}, f32[1536]{0:T(1024)}, u32[]{:S(2)}) copy-start(f32[1536]{0:T(1024)} %get-tuple-element.223) | copy-start | bytes 18436
  63.9 5.5 %copy-start.32 = (f32[1536]{0:T(1024)S(1)}, f32[1536]{0:T(1024)}, u32[]{:S(2)}) copy-start(f32[1536]{0:T(1024)} %get-tuple-element.224) | copy-start | bytes 18436
  64.0 5.5 %copy-start.33 = (f32[1536]{0:T(1024)S(1)}, f32[1536]{0:T(1024)}, u32[]{:S(2)}) copy-start(f32[1536]{0:T(1024)} %get-tuple-element.225) | copy-start | bytes 18436
  64.0 5.5 %copy-start.34 = (f32[1536]{0:T(1024)S(1)}, f32[1536]{0:T(1024)}, u32[]{:S(2)}) copy-start(f32[1536]{0:T(1024)} %get-tuple-element.226) | copy-start | bytes 18436
  64.0 5.5 %copy-start.35 = (f32[1536]{0:T(1024)S(1)}, f32[1536]{0:T(1024)}, u32[]{:S(2)}) copy-start(f32[1536]{0:T(1024)} %get-tuple-element.227) | copy-start | bytes 18436
  64.0 5.5 %copy-start.36 = (f32[1536]{0:T(1024)S(1)}, f32[1536]{0:T(1024)}, u32[]{:S(2)}) copy-start(f32[1536]{0:T(1024)} %get-tuple-element.228) | copy-start | bytes 18436
  64.0 5.5 %copy-start.37 = (f32[1536]{0:T(1024)S(1)}, f32[1536]{0:T(1024)}, u32[]{:S(2)}) copy-start(f32[1536]{0:T(1024)} %get-tuple-element.229) | copy-start | bytes 18436
  64.0 5.5 %copy-start.40 = (pred[128]{0:T(512)(128)(4,1)S(1)}, pred[128]{0:T(512)(128)(4,1)}, u32[]{:S(2)}) copy-start(pred[128]{0:T(512)(128)(4,1)} %get-tuple-element.311) | copy-start | bytes 388
  64.0 5.5 %copy-start.41 = (pred[128]{0:T(512)(128)(4,1)S(1)}, pred[128]{0:T(512)(128)(4,1)}, u32[]{:S(2)}) copy-start(pred[128]{0:T(512)(128)(4,1)} %get-tuple-element.312) | copy-start | bytes 388
  64.0 5.5 %copy-start.42 = (pred[128]{0:T(512)(128)(4,1)S(1)}, pred[128]{0:T(512)(128)(4,1)}, u32[]{:S(2)}) copy-start(pred[128]{0:T(512)(128)(4,1)} %get-tuple-element.313) | copy-start | bytes 388
  64.0 5.5 %copy-start.43 = (pred[128]{0:T(512)(128)(4,1)S(1)}, pred[128]{0:T(512)(128)(4,1)}, u32[]{:S(2)}) copy-start(pred[128]{0:T(512)(128)(4,1)} %get-tuple-element.314) | copy-start | bytes 388
  64.0 5.5 %copy-start.44 = (pred[128]{0:T(512)(128)(4,1)S(1)}, pred[128]{0:T(512)(128)(4,1)}, u32[]{:S(2)}) copy-start(pred[128]{0:T(512)(128)(4,1)} %get-tuple-element.315) | copy-start | bytes 388
  64.1 5.5 %copy-start.45 = (pred[128]{0:T(512)(128)(4,1)S(1)}, pred[128]{0:T(512)(128)(4,1)}, u32[]{:S(2)}) copy-start(pred[128]{0:T(512)(128)(4,1)} %get-tuple-element.316) | copy-start | bytes 388
  64.1 5.5 %copy-start.46 = (pred[128]{0:T(512)(128)(4,1)S(1)}, pred[128]{0:T(512)(128)(4,1)}, u32[]{:S(2)}) copy-start(pred[128]{0:T(512)(128)(4,1)} %get-tuple-element.317) | copy-start | bytes 388
  64.1 5.5 %copy-start.47 = (pred[128]{0:T(512)(128)(4,1)S(1)}, pred[128]{0:T(512)(128)(4,1)}, u32[]{:S(2)}) copy-start(pred[128]{0:T(512)(128)(4,1)} %get-tuple-element.318) | copy-start | bytes 388
  64.1 5.5 %copy-start.48 = (pred[128]{0:T(512)(128)(4,1)S(1)}, pred[128]{0:T(512)(128)(4,1)}, u32[]{:S(2)}) copy-start(pred[128]{0:T(512)(128)(4,1)} %get-tuple-element.319) | copy-start | bytes 388
  96.6 6.2 %copy-start.54 = (pred[128]{0:T(512)(128)(4,1)S(1)}, pred[128]{0:T(512)(128)(4,1)}, u32[]{:S(2)}) copy-start(pred[128]{0:T(512)(128)(4,1)} %get-tuple-element.297) | copy-start | bytes 388
  96.6 6.2 %copy-start.55 = (pred[128]{0:T(512)(128)(4,1)S(1)}, pred[128]{0:T(512)(128)(4,1)}, u32[]{:S(2)}) copy-start(pred[128]{0:T(512)(128)(4,1)} %get-tuple-element.298) | copy-start | bytes 388
  96.6 6.2 %copy-start.56 = (pred[128]{0:T(512)(128)(4,1)S(1)}, pred[128]{0:T(512)(128)(4,1)}, u32[]{:S(2)}) copy-start(pred[128]{0:T(512)(128)(4,1)} %get-tuple-element.299) | copy-start | bytes 388
  97.5 32.0 %collective-permute-start.4 = (bf16[15,1536]{0,1:T(8,128)(2,1)}, bf16[15,1536]{0,1:T(8,128)(2,1)}, u32[]{:S(2)}, u32[]{:S(2)}) collective-permute-start(bf16[15,1536]{0,1:T(8,128)(2,1)} %get-tuple-element.289), channel_id=1, source_target_pairs={{0,1},{1,2},{2,3},{3,4},{4,5},{5,6},{6,7},{7,8},{8,9},{9,10},{10,1... | collective-permute-start | bytes 138248 | tf_op jit(solution)/shard_map/ppermute | solution.py:28
  99.4 30.1 %collective-permute-start.5 = (bf16[15,1536]{0,1:T(8,128)(2,1)S(1)}, bf16[15,1536]{0,1:T(8,128)(2,1)}, u32[]{:S(2)}, u32[]{:S(2)}) collective-permute-start(bf16[15,1536]{0,1:T(8,128)(2,1)S(1)} %get-tuple-element.290), channel_id=1, source_target_pairs={{1,0},{2,1},{3,2},{4,3},{5,4},{6,5},{7,6},{8,7},{9,8},{10,9},{11,1... | collective-permute-start | bytes 138248 | tf_op jit(solution)/shard_map/ppermute | solution.py:30
  131.1 19.2 %copy-start.6 = (f32[1536]{0:T(1024)S(1)}, f32[1536]{0:T(1024)}, u32[]{:S(2)}) copy-start(f32[1536]{0:T(1024)} %param.16) | copy-start | bytes 18436
  131.1 19.2 %copy-start.58 = (f32[128]{0:T(128)S(1)}, f32[128]{0:T(128)}, u32[]{:S(2)}) copy-start(f32[128]{0:T(128)} %copy-done.57) | copy-start | bytes 1540
  131.1 19.2 %copy-start.60 = (f32[128]{0:T(128)S(1)}, f32[128]{0:T(128)}, u32[]{:S(2)}) copy-start(f32[128]{0:T(128)} %copy-done.59) | copy-start | bytes 1540
  199.4 6.8 %copy-start.1 = (f32[128,1536]{0,1:T(8,128)S(1)}, f32[128,1536]{0,1:T(8,128)}, u32[]{:S(2)}) copy-start(f32[128,1536]{0,1:T(8,128)} %get-tuple-element.273) | copy-start | bytes 2359300
  200.9 6.5 %copy-start.38 = (f32[1536]{0:T(1024)S(1)}, f32[1536]{0:T(1024)}, u32[]{:S(2)}) copy-start(f32[1536]{0:T(1024)} %get-tuple-element.198) | copy-start | bytes 18436
  200.9 6.5 %copy-start.39 = (f32[1536]{0:T(1024)S(1)}, f32[1536]{0:T(1024)}, u32[]{:S(2)}) copy-start(f32[1536]{0:T(1024)} %get-tuple-element.195) | copy-start | bytes 18436
  200.9 207.0 %collective-permute-start.6 = (bf16[128,2,1536]{0,2,1:T(8,128)(2,1)}, bf16[128,2,1536]{0,2,1:T(8,128)(2,1)}, u32[]{:S(2)}, u32[]{:S(2)}) collective-permute-start(bf16[128,2,1536]{0,2,1:T(8,128)(2,1)} %get-tuple-element.283), channel_id=1, source_target_pairs={{0,1},{1,2},{2,3},{3,4},{4,5},{5,6},{6,7},{7,8},{8,9},{9,10},{10,1... | collective-permute-start | bytes 2359304 | tf_op jit(solution)/shard_map/ppermute | solution.py:17
  203.5 204.5 %collective-permute-start.7 = (bf16[128,2,1536]{0,2,1:T(8,128)(2,1)}, bf16[128,2,1536]{0,2,1:T(8,128)(2,1)}, u32[]{:S(2)}, u32[]{:S(2)}) collective-permute-start(bf16[128,2,1536]{0,2,1:T(8,128)(2,1)} %get-tuple-element.284), channel_id=1, source_target_pairs={{1,0},{2,1},{3,2},{4,3},{5,4},{6,5},{7,6},{8,7},{9,8},{10,9},{11,1... | collective-permute-start | bytes 2359304 | tf_op jit(solution)/shard_map/ppermute | solution.py:17
  (6 other events, 24.2 us)
Sparse Core Ops, SparseCore 0:
  129.6 276.6 all-reduce.3
where the time goes:
time: 421 us; the launch traced here: 419 us
  blocking collectives  113 us (27%)
  waiting for transfers between devices  89.3 us (21%)
  other arithmetic  70.2 us (17%)
  matrix products  55.7 us (13%)
  local copies, waits for them, and re-layouts  46.8 us (11%)
  starting transfers between devices  27.8 us (7%)
  between operations  15.1 us (4%)
    psum x1, blocking collectives, per_device(): lax.psum((gain_part, kernel_part, bias_part), ('dp', 'seq'))  113 us
    psum x1, waiting for transfers between devices, per_device(): lax.psum((gain_part, kernel_part, bias_part), ('dp', 'seq'))  83.9 us
    reduce_sum x4, other arithmetic, per_device(): jnp.sum(jnp.where(same_taps[tap_index], conv_wide[tap_index:tap_index + f...  29 us
    another operation x32, local copies, waits for them, and re-layouts, per_device(): kernel_part = jnp.stack(kernel_rows, 0)  24.4 us
    reduce_sum x1, other arithmetic, per_device(): gain_part = jnp.sum(grad_in * normed, 0)  19.2 us
    ppermute x4, starting transfers between devices, shifted(): return lax.ppermute(block, axis, route)  16 us
    dot_general x12, matrix products, masked_logits(): jnp.einsum('qhe,khe->hqk', query_rows, key_rows, preferred_element_type=j...  15.4 us
    dot_general x6, matrix products, backward_group(): jnp.einsum('hqk,qhe->khe', grad_logit, query_rows, preferred_element_type...  10.9 us
  transfers between devices with their start and end apart: 9, of which 3 were waited for; matrix products, arithmetic and copies ran while one was open for 27% of the time, Pallas kernels for 0%

commit v1 on v0

--- a/solution.py
+++ b/solution.py
@@ -211,7 +211,8 @@
     key_grad = own_grad[:, 0]
     value_grad = own_grad[:, 1]
     query_grad = from_groups(query_blocks)
-    gain_sum, kernel_sum, bias_sum = lax.psum((gain_part, kernel_part, bias_part), ("dp", "seq"))
+    put_the_modes = lambda vector: jax.lax.psum(jax.lax.psum(vector, "seq"), "dp")
+    gain_sum, kernel_sum, bias_sum = put_the_modes((gain_part, kernel_part, bias_part))
     norm_factor = (lax.axis_size("dp") * lax.axis_size("seq") * frame_count) ** (-0.5)
     return (
         conv_out[None],

time: 421 us -> 588 us (1.40)
  blocking collectives: 113 us -> 270 us
  waiting for transfers between devices: 89.3 us -> 101 us
    psum x1 -> x2, blocking collectives: 113 us -> 270 us  [the longest x1 247 us: per_device(): jax.lax.psum(vector, 'seq')]
    psum x1 -> x2, waiting for transfers between devices: 83.9 us -> 92.6 us  [the longest x1 92.6 us: per_device(): jax.lax.psum(jax.lax.psum(vector, 'seq'), 'dp')]
  transfers between devices with their start and end apart: 9 -> 10, of which waited for: 3 -> 4; matrix products, arithmetic and copies ran while one was open for 27% -> 18% of each run, Pallas kernels for 0% -> 0%
where the time goes in v1:
time: 588 us; the launch traced here: 582 us
  blocking collectives  270 us (46%)
  waiting for transfers between devices  101 us (17%)
  other arithmetic  69.3 us (12%)
  matrix products  50.6 us (9%)
  local copies, waits for them, and re-layouts  47 us (8%)
  starting transfers between devices  27.9 us (5%)
  between operations  15.6 us (3%)
    psum x1, blocking collectives, per_device(): jax.lax.psum(vector, 'seq')  247 us
    psum x1, waiting for transfers between devices, per_device(): jax.lax.psum(jax.lax.psum(vector, 'seq'), 'dp')  92.6 us
    reduce_sum x4, other arithmetic, per_device(): jnp.sum(jnp.where(same_taps[tap_index], conv_wide[tap_index:tap_index + f...  29.1 us
    another operation x32, local copies, waits for them, and re-layouts, per_device(): kernel_part = jnp.stack(kernel_rows, 0)  24.4 us
    psum x1, blocking collectives, per_device(): jax.lax.psum(jax.lax.psum(vector, 'seq'), 'dp')  23.4 us
    reduce_sum x1, other arithmetic, per_device(): gain_part = jnp.sum(grad_in * normed, 0)  16.9 us
    ppermute x4, starting transfers between devices, shifted(): return lax.ppermute(block, axis, route)  16 us
  transfers between devices with their start and end apart: 10, of which 4 were waited for; matrix products, arithmetic and copies ran while one was open for 18% of the time, Pallas kernels for 0%

profile of v1, /device:TPU:1, one launch (start us, length us, event | category | flops | bytes accessed | tf_op | source)
XLA Modules:
  0.0 581.6 jit_solution(11939641245212514185)
XLA Ops:
  7.3 1.3 pad_maximum_fusion.2
  8.5 8.7 %collective-permute-start.1 = (bf16[128,2,1536]{2,0,1:T(8,128)(2,1)S(1)}, bf16[128,2,1536]{2,0,1:T(8,128)(2,1)S(1)}, u32[]{:S(2)}, u32[]{:S(2)}) collective-permute-start(bf16[128,2,1536]{2,0,1:T(8,128)(2,1)S(1)} %pad_maximum_fusion.2), channel_id=1, source_target_pairs={{1,0},{2,1},{3,2},{4,3},{5,4},{6,5},{7,6},{8,7},{9,8},{10,9},{11,1... | collective-permute-start | bytes 2359304 | tf_op jit(solution)/shard_map/ppermute | solution.py:17
  17.3 1.9 collective-permute-start
  23.6 4.5 collective-permute-done
  28.1 1.5 pad_maximum_fusion.1
  29.7 1.6 fusion.197
  31.3 1.8 copy.25
  33.1 1.4 copy.23
  34.6 16.4 %while.28 = (s32[]{:T(128)}, bf16[6,128,4,64]{1,3,2,0:T(8,128)(2,1)S(1)}, f32[6,4,128]{2,1,0:T(4,128)}, bf16[6,384,4,64]{1,3,2,0:T(8,128)(2,1)}, bf16[6,128,4,64...) while((s32[]{:T(128)}, ...), condition=%wide.region_3.4_spmd.clone, body=%wide.region_0.3_spmd.clone.sunk | while | flops 51953152 | bytes 3068009 | solution.py:115
  35.4 1.3 fusion.225
  38.1 1.3 fusion.225
  40.9 1.3 fusion.225
  43.6 1.3 fusion.225
  46.3 1.3 fusion.225
  49.0 1.3 fusion.225
  53.0 4.5 collective-permute-start.2
  57.5 2.1 collective-permute-start.3
  59.6 2.2 slice_reduce_fusion.29
  61.8 1.2 copy.26
  63.4 3.5 collective-permute-done.3
  66.9 1.6 maximum_convert_fusion
  68.8 18.7 %fusion.110 = (f32[1536]{0:T(1024)S(1)}, f32[1536]{0:T(1024)S(1)}, f32[1536]{0:T(1024)S(1)}, f32[1536]{0:T(1024)S(1)}, f32[1536]{0:T(1024)S(1)}, /*index=5*/f32[...) fusion(f32[158,1536]{0,1:T(8,128)S(1)} %maximum_convert_fusion,, ...), kind=kLoop, calls=%fused_computation.158 | loop fusion | flops 25741824 | bytes 26208128 | tf_op jit(solution)/shard_map/reduce_sum | solution.py:143
  87.6 4.4 fusion.112
  92.1 3.7 fusion.114
  96.8 1.9 collective-permute-start.4
  98.7 3.4 collective-permute-start.5
  102.1 2.2 fusion.108
  122.8 6.0 %stack.135 = f32[31,1536]{1,0:T(8,128)} concatenate(f32[1,1536]{1,0:T(1,128)} %stack.104, f32[1,1536]{1,0:T(1,128)} %stack.105, f32[1,1536]{1,0:T(1,128)} %stack.106, f32[1,1536]{1,0:T(1,128)} %stack.107, f32[1,1536]{1,0:T(1,128)} %stack.108, f32[1,1536]{1,0:T(1,128)} %stack.109, f32[1,1536]{1,0:T(1,128)} %stack.110, f32[1,1536]{1,0:T(1,128)} %stack.111, f32[1,1536]{1,0:T(1,128)} %stack.112, ...), dimensions={0} | concatenate | bytes 380928 | tf_op jit(solution)/shard_map/stack | solution.py:152
  129.1 1.6 maximum_convert_fusion.1
  131.1 16.9 %fusion.190 = (f32[1536]{0:T(1024)}, f32[128]{0:T(128)S(1)}, f32[128]{0:T(128)S(1)}, f32[128,1536]{0,1:T(8,128)S(1)}) fusion(bf16[6,128,4,64]{1,3,2,0:T(8,128)(2,1)S(1)} %get-tuple-element.104, f32[128]{0:T(128)} %copy-done.95, f32[128]{0:T(128)} %copy-done.93, f32[1536]{0:T(1024)S(1)} %copy-done.10, f32[158,1536]{0,1:T(8,128)S(1)} %maximum_convert_fusion.1, ...), kind=kLoop, calls=%fused_computation.277 | loop fusion | flops 19855616 | bytes 25767808 | tf_op jit(solution)/shard_map/reduce_sum | solution.py:160
  149.8 45.2 %while.29 = (s32[]{:T(128)}, bf16[6,128,4,64]{1,3,2,0:T(8,128)(2,1)S(1)}, f32[6,384,4,64]{1,3,2,0:T(8,128)}, f32[6,384,4,64]{1,3,2,0:T(8,128)S(1)}, bf16[6,384,4...) while((s32[]{:T(128)}, ...), condition=%wide.region_10.11_spmd.clone, body=%wide.region_9.10_spmd.clone.sunk | while | flops 127451136 | bytes 5426313 | solution.py:192
  150.6 1.3 fusion.237
  151.9 1.3 fusion.238
  153.2 1.2 fusion.239
  155.5 1.8 fusion.240
  158.1 1.3 fusion.237
  159.5 1.3 fusion.238
  160.8 1.2 fusion.239
  163.0 1.8 fusion.240
  165.7 1.3 fusion.237
  167.0 1.3 fusion.238
  168.3 1.2 fusion.239
  170.6 1.8 fusion.240
  173.2 1.3 fusion.237
  174.5 1.3 fusion.238
  175.8 1.2 fusion.239
  178.1 1.8 fusion.240
  180.7 1.3 fusion.237
  182.1 1.3 fusion.238
  183.4 1.2 fusion.239
  185.7 1.8 fusion.240
  188.3 1.3 fusion.237
  189.6 1.3 fusion.238
  190.9 1.2 fusion.239
  193.2 1.8 fusion.240
  195.0 2.0 fusion.48
  197.1 1.5 fusion.196
  198.5 2.5 collective-permute-start.6
  201.1 2.8 collective-permute-start.7
  205.9 246.7 %all-reduce.1 = (f32[1536]{0:T(1024)S(1)}, f32[1536]{0:T(1024)S(1)}) all-reduce(f32[1536]{0:T(1024)S(1)} %copy-done.74, f32[1536]{0:T(1024)S(1)} %copy-done.73), channel_id=1, replica_groups=mesh['dp'=8,'seq'=64] {'seq'}, use_global_device_ids=true, to_apply=%region_12.13 | all-reduce | flops 3072 | bytes 24576 | tf_op jit(solution)/shard_map/psum | solution.py:214
  452.7 23.4 %all-reduce.2 = (f32[1536]{0:T(1024)S(1)}, f32[1536]{0:T(1024)S(1)}) all-reduce(f32[1536]{0:T(1024)S(1)} %get-tuple-element.270, f32[1536]{0:T(1024)S(1)} %get-tuple-element.271), channel_id=1, replica_groups=mesh['dp'=8,'seq'=64] {'dp'}, use_global_device_ids=true, to_apply=%region_13.14 | all-reduce | flops 3072 | bytes 24576 | tf_op jit(solution)/shard_map/psum | solution.py:214
  476.7 92.6 %all-reduce.8.cloned.1.call-done = f32[31,1536]{1,0:T(8,128)} async-done(((f32[31,1536]{1,0:T(8,128)}), f32[31,1536]{1,0:T(8,128)}) %all-reduce.8.cloned.1.call-update) | async-done | bytes 190480 | tf_op jit(solution)/shard_map/psum | solution.py:214
  569.4 1.6 broadcast_multiply_fusion
  571.0 1.9 fusion.52
  (307 shorter events, 52.2 us)
Async XLA Ops:
  7.2 21.0 %copy-start.4 = (bf16[1,128,1536]{2,1,0:T(8,128)(2,1)S(1)}, bf16[1,128,1536]{2,1,0:T(8,128)(2,1)}, u32[]{:S(2)}) copy-start(bf16[1,128,1536]{2,1,0:T(8,128)(2,1)} %param.14) | copy-start | bytes 1179652
  7.2 21.0 %copy-start.5 = (bf16[1,128,1536]{2,1,0:T(8,128)(2,1)S(1)}, bf16[1,128,1536]{2,1,0:T(8,128)(2,1)}, u32[]{:S(2)}) copy-start(bf16[1,128,1536]{2,1,0:T(8,128)(2,1)} %param.13) | copy-start | bytes 1179652
  7.2 12.1 %copy-start.8 = (f32[31,1536]{1,0:T(8,128)S(1)}, f32[31,1536]{1,0:T(8,128)}, u32[]{:S(2)}) copy-start(f32[31,1536]{1,0:T(8,128)} %param.17) | copy-start | bytes 571396
  7.2 13.0 %copy-start.9 = (s32[1,8192]{1,0:T(1,128)S(1)}, s32[1,8192]{1,0:T(1,128)}, u32[]{:S(2)}) copy-start(s32[1,8192]{1,0:T(1,128)} %param.15) | copy-start | bytes 98308
  7.2 13.0 %copy-start.7 = (bf16[1,128,1536]{2,1,0:T(8,128)(2,1)S(1)}, bf16[1,128,1536]{2,1,0:T(8,128)(2,1)}, u32[]{:S(2)}) copy-start(bf16[1,128,1536]{2,1,0:T(8,128)(2,1)} %param.12) | copy-start | bytes 1179652
  7.2 468.9 %all-reduce.6.cloned.1.call-start = ((), (), s32[]{:S(2)}) async-start(), calls=%async_computation | async-start | bytes 393216 | tf_op jit(solution)/shard_map/psum | solution.py:214
  8.5 14.2 %collective-permute-start.1 = (bf16[128,2,1536]{2,0,1:T(8,128)(2,1)S(1)}, bf16[128,2,1536]{2,0,1:T(8,128)(2,1)S(1)}, u32[]{:S(2)}, u32[]{:S(2)}) collective-permute-start(bf16[128,2,1536]{2,0,1:T(8,128)(2,1)S(1)} %pad_maximum_fusion.2), channel_id=1, source_target_pairs={{1,0},{2,1},{3,2},{4,3},{5,4},{6,5},{7,6},{8,7},{9,8},{10,9},{11,1... | collective-permute-start | bytes 2359304 | tf_op jit(solution)/shard_map/ppermute | solution.py:17
  17.3 10.8 %collective-permute-start = (bf16[128,2,1536]{2,0,1:T(8,128)(2,1)S(1)}, bf16[128,2,1536]{2,0,1:T(8,128)(2,1)}, u32[]{:S(2)}, u32[]{:S(2)}) collective-permute-start(bf16[128,2,1536]{2,0,1:T(8,128)(2,1)S(1)} %pad_maximum_fusion.2), channel_id=1, source_target_pairs={{0,1},{1,2},{2,3},{3,4},{4,5},{5,6},{6,7},{7,8},{8,9},{9,10},{10,1... | collective-permute-start | bytes 2359304 | tf_op jit(solution)/shard_map/ppermute | solution.py:17
  34.6 17.1 %copy-start.10 = (f32[1536]{0:T(1024)S(1)}, f32[1536]{0:T(1024)}, u32[]{:S(2)}) copy-start(f32[1536]{0:T(1024)} %param.16) | copy-start | bytes 18436
  51.2 10.6 %copy-start.93 = (f32[128]{0:T(128)}, f32[128]{0:T(128)S(1)}, u32[]{:S(2)}) copy-start(f32[128]{0:T(128)S(1)} %broadcast_multiply_fusion.5) | copy-start | bytes 1540
  51.7 10.1 %copy-start.95 = (f32[128]{0:T(128)}, f32[128]{0:T(128)S(1)}, u32[]{:S(2)}) copy-start(f32[128]{0:T(128)S(1)} %add_rsqrt_fusion) | copy-start | bytes 1540
  53.0 10.4 %collective-permute-start.2 = (bf16[15,1536]{0,1:T(8,128)(2,1)}, bf16[15,1536]{0,1:T(8,128)(2,1)}, u32[]{:S(2)}, u32[]{:S(2)}) collective-permute-start(bf16[15,1536]{0,1:T(8,128)(2,1)} %get-tuple-element.293), channel_id=1, source_target_pairs={{0,1},{1,2},{2,3},{3,4},{4,5},{5,6},{6,7},{7,8},{8,9},{9,10},{10,1... | collective-permute-start | bytes 138248 | tf_op jit(solution)/shard_map/ppermute | solution.py:28
  57.5 9.4 %collective-permute-start.3 = (bf16[15,1536]{0,1:T(8,128)(2,1)}, bf16[15,1536]{0,1:T(8,128)(2,1)}, u32[]{:S(2)}, u32[]{:S(2)}) collective-permute-start(bf16[15,1536]{0,1:T(8,128)(2,1)} %get-tuple-element.294), channel_id=1, source_target_pairs={{1,0},{2,1},{3,2},{4,3},{5,4},{6,5},{7,6},{8,7},{9,8},{10,9},{11,1... | collective-permute-start | bytes 138248 | tf_op jit(solution)/shard_map/ppermute | solution.py:30
  63.0 5.5 copy-start.11
  63.0 5.5 copy-start.13
  63.0 5.5 copy-start.15
  63.0 5.5 copy-start.17
  63.0 5.5 copy-start.19
  63.0 5.5 copy-start.21
  63.0 5.5 copy-start.23
  63.0 5.5 copy-start.25
  63.1 5.5 copy-start.27
  63.1 5.5 copy-start.29
  63.1 5.5 copy-start.31
  63.1 5.5 copy-start.33
  63.1 5.5 copy-start.35
  63.1 5.5 copy-start.37
  63.1 5.5 copy-start.39
  63.1 5.5 copy-start.41
  63.1 5.5 copy-start.43
  63.1 5.5 copy-start.45
  63.2 5.5 copy-start.47
  63.2 5.5 copy-start.49
  63.2 5.5 copy-start.51
  63.2 5.5 copy-start.53
  63.2 5.5 copy-start.55
  63.2 5.5 copy-start.57
  63.2 5.5 copy-start.59
  63.2 5.5 copy-start.61
  63.2 5.5 copy-start.63
  63.2 5.5 copy-start.65
  63.3 5.5 copy-start.67
  63.3 5.5 copy-start.69
  63.3 5.5 copy-start.71
  63.3 5.5 copy-start.75
  63.3 5.5 copy-start.76
  63.3 5.5 copy-start.77
  63.3 5.5 copy-start.78
  63.3 5.5 copy-start.79
  63.3 5.5 copy-start.80
  63.3 5.5 copy-start.81
  95.8 6.2 %copy-start.90 = (pred[128]{0:T(512)(128)(4,1)S(1)}, pred[128]{0:T(512)(128)(4,1)}, u32[]{:S(2)}) copy-start(pred[128]{0:T(512)(128)(4,1)} %get-tuple-element.299) | copy-start | bytes 388
  95.8 6.2 %copy-start.91 = (pred[128]{0:T(512)(128)(4,1)S(1)}, pred[128]{0:T(512)(128)(4,1)}, u32[]{:S(2)}) copy-start(pred[128]{0:T(512)(128)(4,1)} %get-tuple-element.300) | copy-start | bytes 388
  95.8 6.2 %copy-start.92 = (pred[128]{0:T(512)(128)(4,1)S(1)}, pred[128]{0:T(512)(128)(4,1)}, u32[]{:S(2)}) copy-start(pred[128]{0:T(512)(128)(4,1)} %get-tuple-element.301) | copy-start | bytes 388
  96.8 32.4 %collective-permute-start.4 = (bf16[15,1536]{0,1:T(8,128)(2,1)}, bf16[15,1536]{0,1:T(8,128)(2,1)}, u32[]{:S(2)}, u32[]{:S(2)}) collective-permute-start(bf16[15,1536]{0,1:T(8,128)(2,1)} %get-tuple-element.291), channel_id=1, source_target_pairs={{0,1},{1,2},{2,3},{3,4},{4,5},{5,6},{6,7},{7,8},{8,9},{9,10},{10,1... | collective-permute-start | bytes 138248 | tf_op jit(solution)/shard_map/ppermute | solution.py:28
  98.7 30.5 %collective-permute-start.5 = (bf16[15,1536]{0,1:T(8,128)(2,1)S(1)}, bf16[15,1536]{0,1:T(8,128)(2,1)}, u32[]{:S(2)}, u32[]{:S(2)}) collective-permute-start(bf16[15,1536]{0,1:T(8,128)(2,1)S(1)} %get-tuple-element.292), channel_id=1, source_target_pairs={{1,0},{2,1},{3,2},{4,3},{5,4},{6,5},{7,6},{8,7},{9,8},{10,9},{11,1... | collective-permute-start | bytes 138248 | tf_op jit(solution)/shard_map/ppermute | solution.py:30
  128.8 440.6 %all-reduce.8.cloned.1.call-start = ((), (), s32[]{:S(2)}) async-start(), calls=%async_computation.1 | async-start | bytes 393216 | tf_op jit(solution)/shard_map/psum | solution.py:214
  131.0 16.9 %copy-start.94 = (f32[128]{0:T(128)S(1)}, f32[128]{0:T(128)}, u32[]{:S(2)}) copy-start(f32[128]{0:T(128)} %copy-done.93) | copy-start | bytes 1540
  131.0 16.9 %copy-start.96 = (f32[128]{0:T(128)S(1)}, f32[128]{0:T(128)}, u32[]{:S(2)}) copy-start(f32[128]{0:T(128)} %copy-done.95) | copy-start | bytes 1540
  197.0 6.8 %copy-start.2 = (f32[128,1536]{0,1:T(8,128)S(1)}, f32[128,1536]{0,1:T(8,128)}, u32[]{:S(2)}) copy-start(f32[128,1536]{0,1:T(8,128)} %get-tuple-element.275) | copy-start | bytes 2359300
  198.5 7.4 %copy-start.73 = (f32[1536]{0:T(1024)S(1)}, f32[1536]{0:T(1024)}, u32[]{:S(2)}) copy-start(f32[1536]{0:T(1024)} %get-tuple-element.198) | copy-start | bytes 18436
  198.5 7.4 %copy-start.74 = (f32[1536]{0:T(1024)S(1)}, f32[1536]{0:T(1024)}, u32[]{:S(2)}) copy-start(f32[1536]{0:T(1024)} %get-tuple-element.195) | copy-start | bytes 18436
  198.5 372.5 %collective-permute-start.6 = (bf16[128,2,1536]{0,2,1:T(8,128)(2,1)}, bf16[128,2,1536]{0,2,1:T(8,128)(2,1)}, u32[]{:S(2)}, u32[]{:S(2)}) collective-permute-start(bf16[128,2,1536]{0,2,1:T(8,128)(2,1)} %get-tuple-element.285), channel_id=1, source_target_pairs={{0,1},{1,2},{2,3},{3,4},{4,5},{5,6},{6,7},{7,8},{8,9},{9,10},{10,1... | collective-permute-start | bytes 2359304 | tf_op jit(solution)/shard_map/ppermute | solution.py:17
  201.1 369.9 %collective-permute-start.7 = (bf16[128,2,1536]{0,2,1:T(8,128)(2,1)}, bf16[128,2,1536]{0,2,1:T(8,128)(2,1)}, u32[]{:S(2)}, u32[]{:S(2)}) collective-permute-start(bf16[128,2,1536]{0,2,1:T(8,128)(2,1)} %get-tuple-element.286), channel_id=1, source_target_pairs={{1,0},{2,1},{3,2},{4,3},{5,4},{6,5},{7,6},{8,7},{9,8},{10,9},{11,1... | collective-permute-start | bytes 2359304 | tf_op jit(solution)/shard_map/ppermute | solution.py:17
  (43 other events, 102.9 us)
Sparse Core Ops, SparseCore 0:
  128.9 200.1 all-reduce.5
  476.3 93.0 all-reduce.7
